TPU v7x, 32 devices: a whole 2x2x4 slice. The times are simulated.
32 devices in a mesh: dp: 16 (over z, y, x), tensor: 2 (over core).
Axes of the slice: x: 2, y: 2, z: 4, core: 2. Of those that a mesh axis runs over, the one named last changes fastest.
Arguments:
- layer_input: bfloat16 [16, 1024, 1024], P('dp', 'tensor'), may hold values from -6 to 6
- memory: bfloat16 [16, 512, 1024], P('dp', 'tensor'), may hold values from -6 to 6
- evicted: bfloat16 [16, 1536, 1024], P('dp', 'tensor'), may hold values from -6 to 6
- picture_start: int32 [16], P('dp'), may hold values from 0 to 768, as said below
- memory_lengths: int32 [16, 2], P('dp'), may hold values from 128 to 512, as said below
- w_query: bfloat16 [1024, 1024], P('dp', 'tensor'), may hold values from -0.1875 to 0.1875
- w_key: bfloat16 [1024, 1024], P('dp', 'tensor'), may hold values from -0.1875 to 0.1875
- w_value: bfloat16 [1024, 1024], P('dp', 'tensor'), may hold values from -0.1875 to 0.1875
- w_output: bfloat16 [1024, 1024], P('tensor', 'dp'), may hold values from -1.5 to 1.5
- w_compress: bfloat16 [3072, 1024], P(('dp', 'tensor')), may hold values from -0.109375 to 0.109375
- gain_attn: bfloat16 [1024], P(('dp', 'tensor')), may hold values from 0.5 to 1.5
- gain_ffn: bfloat16 [1024], P(('dp', 'tensor')), may hold values from 0.5 to 1.5
- w_inner: bfloat16 [1024, 4096], P('dp', 'tensor'), may hold values from -0.1875 to 0.1875
- w_outer: bfloat16 [4096, 1024], P('tensor', 'dp'), may hold values from -0.09375 to 0.09375
- cotangent: bfloat16 [16, 1024, 1024], P('dp', 'tensor'), may hold values from -6 to 6
Outputs:
- layer_output: bfloat16 [16, 1024, 1024], P('dp', 'tensor')
- input_grad: bfloat16 [16, 1024, 1024], P('dp', 'tensor')
- grad_query: float32 [1024, 1024], P('dp', 'tensor')
- grad_key: float32 [1024, 1024], P('dp', 'tensor')
- grad_value: float32 [1024, 1024], P('dp', 'tensor')
- grad_output_proj: float32 [1024, 1024], P('tensor', 'dp')
- grad_compress: float32 [3072, 1024], P(('dp', 'tensor'))
- grad_gain_attn: float32 [1024], P(('dp', 'tensor'))
- grad_gain_ffn: float32 [1024], P(('dp', 'tensor'))
- grad_inner: float32 [1024, 4096], P('dp', 'tensor')
- grad_outer: float32 [4096, 1024], P('tensor', 'dp')
- branch_rms: float32 [16, 3], P('dp')
Inputs may be any that keep to these rules, and one draw needn't show every extreme that they name: Sequence s treats tokens picture_start[s] to picture_start[s] + 255 as one picture span; starts are multiples of half of 256. `memory_lengths`: column 0 counts the valid most recent rows of memory, column 1 those of compressed memory.
All inputs are finite; a program needn't handle non-finite values.
Results may differ from a plain program's by a relative error of at most 0.018.
Values may be sent and summed in bfloat16 or wider, within the bound.
No kernel may reach another device: no remote copies, remote signals or barrier semaphores. Data moves between devices by JAX's collectives and lax.ppermute only.
A program may use at most 256 MiB of HBM per device.

v0:
```python
import jax
import jax.numpy as jnp
from jax import lax
from jax.sharding import PartitionSpec as P

D = 1024
DH = 128
MEM = 512
CMEM = 512
PIC = 256
L = 1024
epsilon = 1e-06
very_negative = -1e30


def rms_norm(matrix_rows, gain_vec):
    return (
        matrix_rows
        * lax.rsqrt(jnp.mean(matrix_rows * matrix_rows, axis=-1, keepdims=True) + epsilon)
        * gain_vec
    )


def allowed_keys(span_start, valid_lens):
    query_pos = jnp.arange(L, dtype=jnp.int32)[:, None]
    key_pos = jnp.arange(CMEM + MEM + L, dtype=jnp.int32)[None, :]
    comp_ok = (key_pos < CMEM) & (key_pos >= CMEM - valid_lens[1])
    mem_pos = key_pos - CMEM
    mem_ok = (mem_pos >= 0) & (mem_pos < MEM) & (mem_pos >= MEM - valid_lens[0])
    tok_pos = key_pos - CMEM - MEM
    query_pic = (query_pos >= span_start) & (query_pos < span_start + PIC)
    key_pic = (tok_pos >= span_start) & (tok_pos < span_start + PIC)
    tok_ok = (tok_pos >= 0) & ((tok_pos <= query_pos) | query_pic & key_pic)
    return comp_ok | mem_ok | tok_ok


def masked_scores(query_rows, key_rows, span_start, valid_lens):
    allowed = allowed_keys(span_start, valid_lens)
    scores = DH ** (-0.5) * jnp.einsum(
        "qhd,khd->hqk", query_rows, key_rows, preferred_element_type=jnp.float32
    )
    return jnp.where(allowed[None], scores, very_negative)


def attend_one(seq_items):
    query_rows, key_rows, value_rows, span_start, valid_lens = seq_items
    scores = masked_scores(query_rows, key_rows, span_start, valid_lens)
    row_max = jnp.max(scores, axis=-1, keepdims=True)
    shifted = jnp.exp(scores - row_max)
    row_total = jnp.sum(shifted, axis=-1, keepdims=True)
    attn_probs = (shifted / row_total).astype(jnp.bfloat16)
    mixed = jnp.einsum("hqk,khd->qhd", attn_probs, value_rows, preferred_element_type=jnp.float32)
    return (mixed.astype(jnp.bfloat16), row_max + jnp.log(row_total))


def attend_back(seq_items):
    query_rows, key_rows, value_rows, d_mixed, log_total, span_start, valid_lens = seq_items
    scores = masked_scores(query_rows, key_rows, span_start, valid_lens)
    attn_probs = jnp.exp(scores - log_total)
    d_probs = jnp.einsum("qhd,khd->hqk", d_mixed, value_rows, preferred_element_type=jnp.float32)
    d_values = jnp.einsum(
        "hqk,qhd->khd", attn_probs.astype(jnp.bfloat16), d_mixed, preferred_element_type=jnp.float32
    )
    d_scores = (
        attn_probs * (d_probs - jnp.sum(attn_probs * d_probs, axis=-1, keepdims=True))
    ).astype(jnp.bfloat16)
    query_gradient = DH ** (-0.5) * jnp.einsum(
        "hqk,khd->qhd", d_scores, key_rows, preferred_element_type=jnp.float32
    )
    d_keys = DH ** (-0.5) * jnp.einsum(
        "hqk,qhd->khd", d_scores, query_rows, preferred_element_type=jnp.float32
    )
    return (
        query_gradient.astype(jnp.bfloat16),
        d_keys.astype(jnp.bfloat16),
        d_values.astype(jnp.bfloat16),
    )


def to_natural(spread, tensor_size, comp_part, mem_part):
    seq_dev = spread.shape[0]
    feature_dim = spread.shape[-1]
    split_rows = spread.reshape(seq_dev, tensor_size, -1, feature_dim)
    comp_rows = split_rows[:, :, :comp_part].reshape(seq_dev, -1, feature_dim)
    mem_rows = split_rows[:, :, comp_part : comp_part + mem_part].reshape(seq_dev, -1, feature_dim)
    tok_rows = split_rows[:, :, comp_part + mem_part :].reshape(seq_dev, -1, feature_dim)
    return jnp.concatenate([comp_rows, mem_rows, tok_rows], axis=1)


def from_natural(natural, tensor_size, comp_part, mem_part):
    seq_dev = natural.shape[0]
    feature_dim = natural.shape[-1]
    comp_all = tensor_size * comp_part
    mem_all = tensor_size * mem_part
    comp_rows = natural[:, :comp_all].reshape(seq_dev, tensor_size, comp_part, feature_dim)
    mem_rows = natural[:, comp_all : comp_all + mem_all].reshape(
        seq_dev, tensor_size, mem_part, feature_dim
    )
    tok_rows = natural[:, comp_all + mem_all :].reshape(seq_dev, tensor_size, -1, feature_dim)
    return jnp.concatenate([comp_rows, mem_rows, tok_rows], axis=2).reshape(
        seq_dev, -1, feature_dim
    )


def gelu_tanh(inner_in):
    return jax.nn.gelu(inner_in, approximate=True)


def per_device(
    layer_input,
    memory,
    evicted,
    picture_start,
    memory_lengths,
    w_query,
    w_key,
    w_value,
    w_output,
    w_compress,
    gain_attn,
    gain_ffn,
    w_inner,
    w_outer,
    cotangent,
):
    tensor_size = lax.axis_size("tensor")
    seq_dev, part_len, feature_dim = layer_input.shape
    comp_part = evicted.shape[1] // 3
    mem_part = memory.shape[1]
    head_local = w_query.shape[1] // DH
    key_len = CMEM + MEM + L
    compress_full, gain_a_full, gain_f_full = (
        lax.all_gather(w_compress, ("dp", "tensor"), axis=0, tiled=True),
        lax.all_gather(gain_attn, ("dp", "tensor"), axis=0, tiled=True),
        lax.all_gather(gain_ffn, ("dp", "tensor"), axis=0, tiled=True),
    )
    gain_attn_f = gain_a_full.astype(jnp.float32)
    gain_ffn_f = gain_f_full.astype(jnp.float32)
    query_weight, key_w, value_w, output_weight, inner_weight, outer_weight = (
        lax.all_gather(w_query, "dp", axis=0, tiled=True),
        lax.all_gather(w_key, "dp", axis=0, tiled=True),
        lax.all_gather(w_value, "dp", axis=0, tiled=True),
        lax.all_gather(w_output, "dp", axis=1, tiled=True),
        lax.all_gather(w_inner, "dp", axis=0, tiled=True),
        lax.all_gather(w_outer, "dp", axis=1, tiled=True),
    )
    grouped = evicted.reshape(seq_dev, comp_part, 3 * feature_dim)
    compressed = jnp.einsum(
        "sce,ed->scd", grouped, compress_full, preferred_element_type=jnp.float32
    )
    token_f = layer_input.astype(jnp.float32)
    keyed_rows = jnp.concatenate([compressed, memory.astype(jnp.float32), token_f], axis=1)
    attn_value, attn_pull = jax.vjp(rms_norm, keyed_rows, gain_attn_f)
    attn_normed = attn_value.astype(jnp.bfloat16)
    spread_rows = lax.all_gather(attn_normed, "tensor", axis=1, tiled=True)
    natural_rows = to_natural(spread_rows, tensor_size, comp_part, mem_part)
    token_normalized = natural_rows[:, CMEM + MEM :]
    query_rows = jnp.einsum(
        "ujm,mk->ujk", token_normalized, query_weight, preferred_element_type=jnp.float32
    ).astype(jnp.bfloat16)
    key_rows = jnp.einsum(
        "skd,de->ske", natural_rows, key_w, preferred_element_type=jnp.float32
    ).astype(jnp.bfloat16)
    value_rows = jnp.einsum(
        "skd,de->ske", natural_rows, value_w, preferred_element_type=jnp.float32
    ).astype(jnp.bfloat16)
    query_heads = query_rows.reshape(seq_dev, L, head_local, DH)
    key_heads = key_rows.reshape(seq_dev, key_len, head_local, DH)
    value_heads = value_rows.reshape(seq_dev, key_len, head_local, DH)
    mixed_heads, log_total = lax.map(
        attend_one, (query_heads, key_heads, value_heads, picture_start, memory_lengths)
    )
    mixed_flattened = mixed_heads.reshape(seq_dev, L, head_local * DH)
    branch_part = jnp.einsum(
        "avr,ri->avi", mixed_flattened, output_weight, preferred_element_type=jnp.float32
    )
    attn_branch = lax.psum_scatter(
        branch_part.astype(jnp.bfloat16), "tensor", scatter_dimension=1, tiled=True
    ).astype(jnp.float32)
    after_attn = token_f + attn_branch
    ffn_value, ffn_pull = jax.vjp(rms_norm, after_attn, gain_ffn_f)
    ffn_normed = ffn_value.astype(jnp.bfloat16)
    feedforward_rows = lax.all_gather(ffn_normed, "tensor", axis=1, tiled=True)
    inner_hidden = jnp.einsum(
        "qmy,yx->qmx", feedforward_rows, inner_weight, preferred_element_type=jnp.float32
    )
    active_f, gelu_pull = jax.vjp(gelu_tanh, inner_hidden)
    hidden_active = active_f.astype(jnp.bfloat16)
    feedforward_share = jnp.einsum(
        "qwh,hj->qwj", hidden_active, outer_weight, preferred_element_type=jnp.float32
    )
    ffn_branch = lax.psum_scatter(
        feedforward_share.astype(jnp.bfloat16), "tensor", scatter_dimension=1, tiled=True
    ).astype(jnp.float32)
    summed = after_attn + ffn_branch
    layer_output = summed.astype(jnp.bfloat16)
    square_sums = jnp.stack(
        [
            jnp.sum(attn_branch * attn_branch, axis=(1, 2)),
            jnp.sum(ffn_branch * ffn_branch, axis=(1, 2)),
            jnp.sum(summed * summed, axis=(1, 2)),
        ],
        axis=1,
    )
    incoming_row_grads = lax.all_gather(cotangent, "tensor", axis=1, tiled=True)
    active_gradient = jnp.einsum(
        "wve,ne->wvn", incoming_row_grads, outer_weight, preferred_element_type=jnp.float32
    )
    grad_outer_part = jnp.einsum(
        "wkz,wky->zy", hidden_active, incoming_row_grads, preferred_element_type=jnp.float32
    )
    inner_gradient = gelu_pull(active_gradient)[0].astype(jnp.bfloat16)
    grad_inner_part = jnp.einsum(
        "vea,vem->am", feedforward_rows, inner_gradient, preferred_element_type=jnp.float32
    )
    feedforward_row_gradient = jnp.einsum(
        "tar,br->tab", inner_gradient, inner_weight, preferred_element_type=jnp.float32
    )
    tiled_sums = jnp.tile(square_sums, (1, tensor_size))
    d_ffn_normed, seq_sums = (
        lax.psum_scatter(
            feedforward_row_gradient.astype(jnp.bfloat16), "tensor", scatter_dimension=1, tiled=True
        ).astype(jnp.float32),
        lax.psum_scatter(
            tiled_sums.astype(jnp.bfloat16), "tensor", scatter_dimension=1, tiled=True
        ).astype(jnp.float32),
    )
    branch_rms = jnp.sqrt(seq_sums / (L * D))
    d_after, grad_gain_ffn_part = ffn_pull(d_ffn_normed)
    grad_after = cotangent.astype(jnp.float32) + d_after
    incoming_attention_grad = lax.all_gather(
        grad_after.astype(jnp.bfloat16), "tensor", axis=1, tiled=True
    )
    d_mixed = jnp.einsum(
        "gqa,ba->gqb", incoming_attention_grad, output_weight, preferred_element_type=jnp.float32
    ).astype(jnp.bfloat16)
    grad_output_part = jnp.einsum(
        "knm,knc->mc", mixed_flattened, incoming_attention_grad, preferred_element_type=jnp.float32
    )
    query_gradient, d_keys, d_values = lax.map(
        attend_back,
        (
            query_heads,
            key_heads,
            value_heads,
            d_mixed.reshape(seq_dev, L, head_local, DH),
            log_total,
            picture_start,
            memory_lengths,
        ),
    )
    query_gradient = query_gradient.reshape(seq_dev, L, head_local * DH)
    d_keys = d_keys.reshape(seq_dev, key_len, head_local * DH)
    d_values = d_values.reshape(seq_dev, key_len, head_local * DH)
    grad_query_part = jnp.einsum(
        "frk,frj->kj", token_normalized, query_gradient, preferred_element_type=jnp.float32
    )
    grad_key_part = jnp.einsum(
        "skd,ske->de", natural_rows, d_keys, preferred_element_type=jnp.float32
    )
    grad_value_part = jnp.einsum(
        "skd,ske->de", natural_rows, d_values, preferred_element_type=jnp.float32
    )
    d_natural = jnp.einsum(
        "ske,de->skd", d_keys, key_w, preferred_element_type=jnp.float32
    ) + jnp.einsum("ske,de->skd", d_values, value_w, preferred_element_type=jnp.float32)
    token_gradient = jnp.einsum(
        "iuo,co->iuc", query_gradient, query_weight, preferred_element_type=jnp.float32
    )
    d_natural = jnp.concatenate(
        [d_natural[:, : CMEM + MEM], d_natural[:, CMEM + MEM :] + token_gradient], axis=1
    )
    d_spread = from_natural(d_natural, tensor_size, comp_part, mem_part)
    d_attn_normed = lax.psum_scatter(
        d_spread.astype(jnp.bfloat16), "tensor", scatter_dimension=1, tiled=True
    ).astype(jnp.float32)
    d_keyed, grad_gain_attn_part = attn_pull(d_attn_normed)
    input_grad = (grad_after + d_keyed[:, comp_part + mem_part :]).astype(jnp.bfloat16)
    d_compressed = d_keyed[:, :comp_part].astype(jnp.bfloat16)
    grad_compress_part = jnp.einsum(
        "sce,scd->ed", grouped, d_compressed, preferred_element_type=jnp.float32
    )
    grad_compress, grad_gain_attn, grad_gain_ffn = (
        lax.psum_scatter(grad_compress_part, ("dp", "tensor"), scatter_dimension=0, tiled=True),
        lax.psum_scatter(grad_gain_attn_part, ("dp", "tensor"), scatter_dimension=0, tiled=True),
        lax.psum_scatter(grad_gain_ffn_part, ("dp", "tensor"), scatter_dimension=0, tiled=True),
    )
    grad_query, grad_key, grad_value, grad_output_proj, grad_inner, grad_outer = (
        lax.psum_scatter(grad_query_part, "dp", scatter_dimension=0, tiled=True),
        lax.psum_scatter(grad_key_part, "dp", scatter_dimension=0, tiled=True),
        lax.psum_scatter(grad_value_part, "dp", scatter_dimension=0, tiled=True),
        lax.psum_scatter(grad_output_part, "dp", scatter_dimension=1, tiled=True),
        lax.psum_scatter(grad_inner_part, "dp", scatter_dimension=0, tiled=True),
        lax.psum_scatter(grad_outer_part, "dp", scatter_dimension=1, tiled=True),
    )
    return (
        layer_output,
        input_grad,
        grad_query,
        grad_key,
        grad_value,
        grad_output_proj,
        grad_compress,
        grad_gain_attn,
        grad_gain_ffn,
        grad_inner,
        grad_outer,
        branch_rms,
    )


def solution(mesh):
    in_specs = (
        P("dp", "tensor", None),
        P("dp", "tensor", None),
        P("dp", "tensor", None),
        P("dp"),
        P("dp", None),
        P("dp", "tensor"),
        P("dp", "tensor"),
        P("dp", "tensor"),
        P("tensor", "dp"),
        P(("dp", "tensor"), None),
        P(("dp", "tensor")),
        P(("dp", "tensor")),
        P("dp", "tensor"),
        P("tensor", "dp"),
        P("dp", "tensor", None),
    )
    out_specs = (
        P("dp", "tensor", None),
        P("dp", "tensor", None),
        P("dp", "tensor"),
        P("dp", "tensor"),
        P("dp", "tensor"),
        P("tensor", "dp"),
        P(("dp", "tensor"), None),
        P(("dp", "tensor")),
        P(("dp", "tensor")),
        P("dp", "tensor"),
        P("tensor", "dp"),
        P("dp", None),
    )
    return jax.shard_map(
        per_device, mesh=mesh, in_specs=in_specs, out_specs=out_specs, check_vma=False
    )
```

profile of v0, /device:TPU:0, one launch (start us, length us, event | category | flops | bytes accessed | tf_op | source)
XLA Modules:
  0.0 1562.3 jit_solution(4644787308819729858)
XLA Ops:
  9.7 42.9 %all-reduce.6 = (bf16[1024]{0:T(1024)(128)(2,1)S(1)}, bf16[1024]{0:T(1024)(128)(2,1)S(1)}) all-reduce(bf16[1024]{0:T(1024)(128)(2,1)S(1)} %dynamic-update-slice.1, bf16[1024]{0:T(1024)(128)(2,1)S(1)} %dynamic-update-slice), channel_id=1, replica_groups=mesh['dp'=16,'tensor'=2] {'dp','tensor'}, use_global_device_ids=true, to_apply=%add.1 | all-reduce | flops 2048 | bytes 8192
  54.7 3.7 reshape.678
  58.7 24.3 %all-gather.12.cloned.1.call-done = bf16[3072,1024]{1,0:T(8,128)(2,1)} async-done(((bf16[96,1024]{1,0:T(8,128)(2,1)}), bf16[3072,1024]{1,0:T(8,128)(2,1)}) %all-gather.12.cloned.1.call-update) | async-done | bytes 6291472 | tf_op jit(solution)/shard_map/all_gather | solution.py:133
  83.0 5.1 convolution_bitcast_fusion.1
  97.2 4.2 fusion.15
  108.3 54.7 %all-gather.18.cloned.1.call-done = bf16[1024,512]{1,0:T(8,128)(2,1)} async-done(((bf16[64,512]{1,0:T(8,128)(2,1)}), bf16[1024,512]{1,0:T(8,128)(2,1)}) %all-gather.18.cloned.1.call-update) | async-done | bytes 1048592 | tf_op jit(solution)/shard_map/all_gather | solution.py:140
  163.0 3.5 convolution_convert_fusion.2
  166.5 53.1 %all-gather.20.cloned.1.call-done = bf16[1024,512]{1,0:T(8,128)(2,1)} async-done(((bf16[64,512]{1,0:T(8,128)(2,1)}), bf16[1024,512]{1,0:T(8,128)(2,1)}) %all-gather.20.cloned.1.call-update) | async-done | bytes 1048592 | tf_op jit(solution)/shard_map/all_gather | solution.py:141
  219.5 4.4 convolution_convert_fusion
  224.0 16.4 %fusion.75 = (f32[4,1024]{1,0:T(4,128)S(1)}, f32[4,1024,2048]{2,1,0:T(8,128)}) fusion(bf16[1024,4,128]{0,2,1:T(8,128)(2,1)} %bitcast.143, bf16[2048,4,128]{0,2,1:T(8,128)(2,1)S(1)} %bitcast.125, pred[1024,2048]{1,0:T(8,128)(4,1)S(1)} %copy-done.23), kind=kOutput, calls=%fused_computation.122 | convolution fusion | flops 2172645376 | bytes 38813696 | tf_op jit(solution)/shard_map/while/body/eval_jaxpr/qhd,khd->hqk/dot_general | solution.py:39
  240.4 13.8 fusion
  254.2 21.9 %all-gather.16.cloned.1.call-done = bf16[1024,512]{1,0:T(8,128)(2,1)} async-done(((bf16[64,512]{1,0:T(8,128)(2,1)}), bf16[1024,512]{1,0:T(8,128)(2,1)}) %all-gather.16.cloned.1.call-update) | async-done | bytes 1048592 | tf_op jit(solution)/shard_map/all_gather | solution.py:142
  276.1 4.9 convolution_convert_fusion.1
  281.0 15.7 %fusion.49 = bf16[4,128,1024]{2,1,0:T(8,128)(2,1)} fusion(bf16[2048,4,128]{0,2,1:T(8,128)(2,1)S(1)} %bitcast.133, f32[4,1024,2048]{2,1,0:T(8,128)} %get-tuple-element.112, f32[4,1024]{1,0:T(4,128)S(1)} %fusion, f32[4,1024]{1,0:T(4,128)S(1)} %get-tuple-element.111), kind=kOutput, calls=%fused_computation.82 | convolution fusion | flops 2173173760 | bytes 36732928 | tf_op jit(solution)/shard_map/while/body/eval_jaxpr/hqk,khd->qhd/dot_general | solution.py:52
  296.7 36.0 %all-gather.22.cloned.1.call-done = bf16[512,1024]{0,1:T(8,128)(2,1)} async-done(((bf16[512,64]{0,1:T(8,128)(2,1)}), bf16[512,1024]{0,1:T(8,128)(2,1)}) %all-gather.22.cloned.1.call-update) | async-done | bytes 1048592 | tf_op jit(solution)/shard_map/all_gather | solution.py:143
  332.7 4.2 convert_bitcast_fusion.2
  337.7 7.9 reduce-scatter.15.cloned.1.call-done
  351.2 74.1 %all-gather.26.cloned.1.call-done = bf16[1024,2048]{1,0:T(8,128)(2,1)} async-done(((bf16[64,2048]{1,0:T(8,128)(2,1)}), bf16[1024,2048]{1,0:T(8,128)(2,1)}) %all-gather.26.cloned.1.call-update) | async-done | bytes 4194320 | tf_op jit(solution)/shard_map/all_gather | solution.py:144
  425.3 11.3 all-gather.24.cloned.1.call-done
  436.6 11.0 fusion.44
  449.8 79.6 %all-gather.28.cloned.1.call-done = bf16[2048,1024]{0,1:T(8,128)(2,1)} async-done(((bf16[2048,64]{0,1:T(8,128)(2,1)}), bf16[2048,1024]{0,1:T(8,128)(2,1)}) %all-gather.28.cloned.1.call-update) | async-done | bytes 4194320 | tf_op jit(solution)/shard_map/all_gather | solution.py:145
  529.4 12.7 fusion.12
  544.1 5.8 convert_bitcast_fusion
  550.0 11.2 convert_bitcast_fusion.1
  561.6 10.1 reduce-scatter.17.cloned.1.call-done
  571.7 5.2 fusion.29
  579.4 11.9 all-gather.32.cloned.1.call-done
  591.3 3.1 fusion.46
  594.5 13.7 fusion.21
  608.3 22.0 %multiply_reduce_fusion = (f32[4,1024]{1,0:T(4,128)S(1)}, f32[4,1024,2048]{2,1,0:T(8,128)}) fusion(f32[4,1024,2048]{2,1,0:T(8,128)} %get-tuple-element.112, f32[4,1024]{1,0:T(4,128)S(1)} %log_add_fusion, bf16[1024,4,128]{0,2,1:T(8,128)(2,1)S(1)} %bitcast.128, bf16[2048,4,128]{0,2,1:T(8,128)(2,1)S(1)} %bitcast.134), kind=kOutput, calls=%fused_computation.1 | convolution fusion | flops 2172645376 | bytes 70287360 | tf_op jit(solution)/shard_map/while/body/eval_jaxpr/qhd,khd->hqk/dot_general | solution.py:60
  630.3 27.9 %multiply_convert_fusion = bf16[4,1024,2048]{2,1,0:T(8,128)(2,1)} fusion(f32[4,1024,2048]{2,1,0:T(8,128)} %get-tuple-element.114, f32[4,1024,2048]{2,1,0:T(8,128)} %get-tuple-element.112, f32[4,1024]{1,0:T(4,128)S(1)} %get-tuple-element.113, f32[4,1024]{1,0:T(4,128)S(1)} %log_add_fusion), kind=kLoop, calls=%fused_computation | loop fusion | flops 33554432 | bytes 83918848 | tf_op jit(solution)/shard_map/while/body/eval_jaxpr/convert_element_type | solution.py:66
  658.2 12.1 multiply_convert_fusion.4
  670.3 8.6 multiply_convert_fusion.2
  688.9 4.6 fusion.32
  693.6 5.9 fusion.70
  699.6 7.2 fusion.71
  709.8 12.0 fusion.36
  723.4 9.0 fusion.42
  741.2 6.4 convolution_bitcast_fusion
  747.6 12.7 copy.41
  767.3 41.1 %all-reduce.5 = (f32[1024]{0:T(1024)S(1)}, f32[1024]{0:T(1024)S(1)}) all-reduce(f32[1024]{0:T(1024)S(1)} %get-tuple-element.93, f32[1024]{0:T(1024)S(1)} %copy-done.38), channel_id=11, replica_groups=mesh['dp'=16,'tensor'=2] {'dp','tensor'}, use_global_device_ids=true, to_apply=%region_17.18.clone | all-reduce | flops 2048 | bytes 16384
  809.7 3.7 fusion.31
  813.4 55.1 %reduce-scatter.27.cloned.1.call-done = f32[64,512]{1,0:T(8,128)} async-done(((f32[1024,512]{1,0:T(8,128)}), f32[64,512]{1,0:T(8,128)}) %reduce-scatter.27.cloned.1.call-update) | async-done | bytes 131088 | tf_op jit(solution)/shard_map/reduce_scatter | solution.py:291
  868.5 81.0 %reduce-scatter.25.cloned.1.call-done = f32[64,512]{1,0:T(8,128)} async-done(((f32[1024,512]{1,0:T(8,128)}), f32[64,512]{1,0:T(8,128)}) %reduce-scatter.25.cloned.1.call-update) | async-done | bytes 131088 | tf_op jit(solution)/shard_map/reduce_scatter | solution.py:290
  949.5 81.0 %reduce-scatter.23.cloned.1.call-done = f32[64,512]{1,0:T(8,128)} async-done(((f32[1024,512]{1,0:T(8,128)}), f32[64,512]{1,0:T(8,128)}) %reduce-scatter.23.cloned.1.call-update) | async-done | bytes 131088 | tf_op jit(solution)/shard_map/reduce_scatter | solution.py:289
  1030.4 177.4 %reduce-scatter.33.cloned.1.call-done = f32[2048,64]{0,1:T(8,128)} async-done(((f32[2048,1024]{0,1:T(8,128)}), f32[2048,64]{0,1:T(8,128)}) %reduce-scatter.33.cloned.1.call-update) | async-done | bytes 524304 | tf_op jit(solution)/shard_map/reduce_scatter | solution.py:294
  1207.9 183.2 %reduce-scatter.31.cloned.1.call-done = f32[64,2048]{1,0:T(8,128)} async-done(((f32[1024,2048]{1,0:T(8,128)}), f32[64,2048]{1,0:T(8,128)}) %reduce-scatter.31.cloned.1.call-update) | async-done | bytes 524304 | tf_op jit(solution)/shard_map/reduce_scatter | solution.py:293
  1391.1 163.9 %reduce-scatter.35.cloned.1.call-done = f32[96,1024]{1,0:T(8,128)} async-done(((f32[3072,1024]{1,0:T(8,128)}), f32[96,1024]{1,0:T(8,128)}) %reduce-scatter.35.cloned.1.call-update) | async-done | bytes 393232
  (180 shorter events, 63.2 us)
Async XLA Ops:
  7.2 51.3 %copy-start.2 = (bf16[1,512,1024]{2,1,0:T(8,128)(2,1)S(1)}, bf16[1,512,1024]{2,1,0:T(8,128)(2,1)}, u32[]{:S(2)}) copy-start(bf16[1,512,1024]{2,1,0:T(8,128)(2,1)} %param.15) | copy-start | bytes 3145732
  7.2 75.9 %all-gather.12.cloned.1.call-start = ((), (), s32[]{:S(2)}) async-start(), calls=%async_computation.11 | async-start | bytes 6488064 | tf_op jit(solution)/shard_map/all_gather | solution.py:133
  7.9 96.0 %all-gather.14.cloned.1.call-start = ((), (), s32[]{:S(2)}) async-start(), calls=%async_computation.12 | async-start | bytes 6291456 | tf_op jit(solution)/shard_map/all_gather | solution.py:155
  52.6 36.5 %copy-start.28 = (f32[1024]{0:T(1024)}, f32[1024]{0:T(1024)S(1)}, u32[]{:S(2)}) copy-start(f32[1024]{0:T(1024)S(1)} %convert_element_type.166) | copy-start | bytes 12292
  58.7 30.4 %copy-start = (f32[1,512,1024]{2,1,0:T(8,128)}, f32[1,512,1024]{2,1,0:T(8,128)S(1)}, u32[]{:S(2)}) copy-start(f32[1,512,1024]{2,1,0:T(8,128)S(1)} %convert_element_type.164) | copy-start | bytes 6291460
  83.0 5.1 copy-start.6
  89.8 5.5 copy-start.39
  91.6 71.4 %all-gather.18.cloned.1.call-start = ((), (), s32[]{:S(2)}) async-start(), calls=%async_computation.14 | async-start | bytes 1114112 | tf_op jit(solution)/shard_map/all_gather | solution.py:140
  92.3 127.2 %all-gather.20.cloned.1.call-start = ((), (), s32[]{:S(2)}) async-start(), calls=%async_computation.15 | async-start | bytes 1114112 | tf_op jit(solution)/shard_map/all_gather | solution.py:141
  92.9 183.2 %all-gather.16.cloned.1.call-start = ((), (), s32[]{:S(2)}) async-start(), calls=%async_computation.13 | async-start | bytes 1114112 | tf_op jit(solution)/shard_map/all_gather | solution.py:142
  93.5 239.2 %all-gather.22.cloned.1.call-start = ((), (), s32[]{:S(2)}) async-start(), calls=%async_computation.16 | async-start | bytes 1114112 | tf_op jit(solution)/shard_map/all_gather | solution.py:143
  94.0 251.6 %reduce-scatter.15.cloned.1.call-start = ((), (), s32[]{:S(2)}) async-start(), calls=%async_computation.17 | async-start | bytes 3145728 | tf_op jit(solution)/shard_map/reduce_scatter | solution.py:177
  106.7 112.8 %copy-start.21 = (bf16[1,2,512,1024]{3,2,1,0:T(8,128)(2,1)}, bf16[1,2,512,1024]{3,2,1,0:T(8,128)(2,1)S(1)}, u32[]{:S(2)}) copy-start(bf16[1,2,512,1024]{3,2,1,0:T(8,128)(2,1)S(1)} %slice.56) | copy-start | bytes 6291460
  219.5 4.4 copy-start.23
  223.9 16.4 %copy-start.16 = (bf16[2048,512]{0,1:T(8,128)(2,1)}, bf16[2048,512]{0,1:T(8,128)(2,1)S(1)}, u32[]{:S(2)}) copy-start(bf16[2048,512]{0,1:T(8,128)(2,1)S(1)} %convolution_convert_fusion) | copy-start | bytes 6291460
  281.0 15.7 %copy-start.18 = (bf16[2048,512]{0,1:T(8,128)(2,1)}, bf16[2048,512]{0,1:T(8,128)(2,1)S(1)}, u32[]{:S(2)}) copy-start(bf16[2048,512]{0,1:T(8,128)(2,1)S(1)} %convolution_convert_fusion.1) | copy-start | bytes 6291460
  336.8 88.4 %all-gather.26.cloned.1.call-start = ((), (), s32[]{:S(2)}) async-start(), calls=%async_computation.19 | async-start | bytes 4456448 | tf_op jit(solution)/shard_map/all_gather | solution.py:144
  337.6 99.0 %all-gather.24.cloned.1.call-start = ((), (), s32[]{:S(2)}) async-start(), calls=%async_computation.18 | async-start | bytes 3145728 | tf_op jit(solution)/shard_map/all_gather | solution.py:183
  337.7 239.3 %copy-start.26 = (f32[1024]{0:T(1024)}, f32[1024]{0:T(1024)S(1)}, u32[]{:S(2)}) copy-start(f32[1024]{0:T(1024)S(1)} %convert_element_type.177) | copy-start | bytes 12292
  347.2 229.7 %copy-start.32 = (f32[512]{0:T(512)}, f32[512]{0:T(512)S(1)}, u32[]{:S(2)}) copy-start(f32[512]{0:T(512)S(1)} %fusion.66) | copy-start | bytes 6148
  349.8 99.9 %all-gather.30.cloned.1.call-start = ((), (), s32[]{:S(2)}) async-start(), calls=%async_computation.22 | async-start | bytes 3145728 | tf_op jit(solution)/shard_map/all_gather | solution.py:205
  350.4 178.9 %all-gather.28.cloned.1.call-start = ((), (), s32[]{:S(2)}) async-start(), calls=%async_computation.20 | async-start | bytes 4456448 | tf_op jit(solution)/shard_map/all_gather | solution.py:145
  351.2 210.5 %reduce-scatter.19.cloned.1.call-start = ((), (), s32[]{:S(2)}) async-start(), calls=%async_computation.23 | async-start | bytes 3145728 | tf_op jit(solution)/shard_map/reduce_scatter | solution.py:221
  529.3 14.8 copy-start.40
  549.9 21.8 %copy-start.4 = (bf16[1,512,1024]{2,1,0:T(8,128)(2,1)S(1)}, bf16[1,512,1024]{2,1,0:T(8,128)(2,1)}, u32[]{:S(2)}) copy-start(bf16[1,512,1024]{2,1,0:T(8,128)(2,1)} %reduce-scatter.15.cloned.1.call-done) | copy-start | bytes 3145732
  549.9 21.8 %reduce-scatter.17.cloned.1.call-start = ((), (), s32[]{:S(2)}) async-start(), calls=%async_computation.21 | async-start | bytes 3145728 | tf_op jit(solution)/shard_map/reduce_scatter | solution.py:192
  561.1 16.4 %copy-start.11 = (bf16[1,512,1024]{2,1,0:T(8,128)(2,1)S(1)}, bf16[1,512,1024]{2,1,0:T(8,128)(2,1)}, u32[]{:S(2)}) copy-start(bf16[1,512,1024]{2,1,0:T(8,128)(2,1)} %param.29) | copy-start | bytes 3145732
  561.2 30.2 %all-gather.32.cloned.1.call-start = ((), (), s32[]{:S(2)}) async-start(), calls=%async_computation.24 | async-start | bytes 3145728 | tf_op jit(solution)/shard_map/all_gather | solution.py:231
  571.7 5.8 copy-start.13
  579.3 153.2 %reduce-scatter.21.cloned.1.call-start = ((), (), s32[]{:S(2)}) async-start(), calls=%async_computation.25 | async-start | bytes 6291456 | tf_op jit(solution)/shard_map/reduce_scatter | solution.py:274
  594.5 13.8 copy-start.19
  670.3 8.6 copy-start.42
  688.9 124.5 %reduce-scatter.29.cloned.1.call-start = ((), (), s32[]{:S(2)}) async-start(), calls=%async_computation.29 | async-start | bytes 2228224 | tf_op jit(solution)/shard_map/reduce_scatter | solution.py:292
  693.6 174.9 %reduce-scatter.27.cloned.1.call-start = ((), (), s32[]{:S(2)}) async-start(), calls=%async_computation.28 | async-start | bytes 2228224 | tf_op jit(solution)/shard_map/reduce_scatter | solution.py:291
  699.5 7.3 copy-start.22
  699.5 249.9 %reduce-scatter.25.cloned.1.call-start = ((), (), s32[]{:S(2)}) async-start(), calls=%async_computation.27 | async-start | bytes 2228224 | tf_op jit(solution)/shard_map/reduce_scatter | solution.py:290
  706.8 323.7 %reduce-scatter.23.cloned.1.call-start = ((), (), s32[]{:S(2)}) async-start(), calls=%async_computation.26 | async-start | bytes 2228224 | tf_op jit(solution)/shard_map/reduce_scatter | solution.py:289
  709.5 498.4 %reduce-scatter.33.cloned.1.call-start = ((), (), s32[]{:S(2)}) async-start(), calls=%async_computation.31 | async-start | bytes 8912896 | tf_op jit(solution)/shard_map/reduce_scatter | solution.py:294
  721.8 669.3 %reduce-scatter.31.cloned.1.call-start = ((), (), s32[]{:S(2)}) async-start(), calls=%async_computation.30 | async-start | bytes 8912896 | tf_op jit(solution)/shard_map/reduce_scatter | solution.py:293
  732.5 5.0 copy-start.35
  732.5 822.5 %reduce-scatter.35.cloned.1.call-start = ((), (), s32[]{:S(2)}) async-start(), calls=%async_computation.32 | async-start | bytes 12976128
  760.3 7.1 copy-start.38
  760.3 49.4 %copy-start.3 = (bf16[1,512,1024]{2,1,0:T(8,128)(2,1)S(1)}, bf16[1,512,1024]{2,1,0:T(8,128)(2,1)}, u32[]{:S(2)}) copy-start(bf16[1,512,1024]{2,1,0:T(8,128)(2,1)} %param.15) | copy-start | bytes 3145732
  760.3 49.4 %copy-start.5 = (bf16[1,512,1024]{2,1,0:T(8,128)(2,1)S(1)}, bf16[1,512,1024]{2,1,0:T(8,128)(2,1)}, u32[]{:S(2)}) copy-start(bf16[1,512,1024]{2,1,0:T(8,128)(2,1)} %reduce-scatter.15.cloned.1.call-done) | copy-start | bytes 3145732
  760.3 49.4 %copy-start.12 = (bf16[1,512,1024]{2,1,0:T(8,128)(2,1)S(1)}, bf16[1,512,1024]{2,1,0:T(8,128)(2,1)}, u32[]{:S(2)}) copy-start(bf16[1,512,1024]{2,1,0:T(8,128)(2,1)} %param.29) | copy-start | bytes 3145732
  760.3 49.3 %copy-start.27 = (f32[1024]{0:T(1024)S(1)}, f32[1024]{0:T(1024)}, u32[]{:S(2)}) copy-start(f32[1024]{0:T(1024)} %copy-done.26) | copy-start | bytes 12292
  760.3 49.3 %copy-start.33 = (f32[512]{0:T(512)S(1)}, f32[512]{0:T(512)}, u32[]{:S(2)}) copy-start(f32[512]{0:T(512)} %copy-done.32) | copy-start | bytes 6148
  760.3 49.3 %copy-start.37 = (f32[512]{0:T(512)S(1)}, f32[512]{0:T(512)}, u32[]{:S(2)}) copy-start(f32[512]{0:T(512)} %copy-done.36) | copy-start | bytes 6148
  (19 other events, 35.3 us)
Sparse Core Ops, SparseCore 0:
  10.9 72.1 all-gather.11
  91.7 12.1 all-gather.13
  106.7 56.2 all-gather.17
  165.6 53.9 all-gather.19
  222.1 53.8 all-gather.15
  278.7 53.9 all-gather.21
  337.0 8.5 reduce-scatter.14
  348.3 76.8 all-gather.25
  427.4 9.1 all-gather.23
  438.0 11.7 all-gather.29
  452.5 76.7 all-gather.27
  550.0 8.3 reduce-scatter.18
  561.3 10.3 reduce-scatter.16
  579.5 11.8 all-gather.31
  689.0 13.2 reduce-scatter.20
  705.0 82.7 reduce-scatter.28
  790.5 77.9 reduce-scatter.26
  871.2 78.2 reduce-scatter.24
  952.3 78.0 reduce-scatter.22
  1033.2 174.6 reduce-scatter.32
  1210.8 180.2 reduce-scatter.30
  1397.7 157.2 reduce-scatter.34
where the time goes:
time: 1570 us; the launch traced here: 1560 us
  waiting for transfers between devices  1140 us (73%)
  matrix products  209 us (13%)
  blocking collectives  86.5 us (6%)
  other arithmetic  75.1 us (5%)
  local copies, waits for them, and re-layouts  35.8 us (2%)
  between operations  18 us (1%)
    reduce_scatter x1, waiting for transfers between devices, per_device(): lax.psum_scatter(grad_inner_part, 'dp', scatter_dimension=0, tiled=True)  183 us
    reduce_scatter x1, waiting for transfers between devices, per_device(): lax.psum_scatter(grad_outer_part, 'dp', scatter_dimension=1, tiled=True)  177 us
    unnamed x23, waiting for transfers between devices  169 us
    unnamed x3, blocking collectives  86.5 us
    reduce_scatter x1, waiting for transfers between devices, per_device(): lax.psum_scatter(grad_query_part, 'dp', scatter_dimension=0, tiled=True)  81 us
    reduce_scatter x1, waiting for transfers between devices, per_device(): lax.psum_scatter(grad_key_part, 'dp', scatter_dimension=0, tiled=True)  81 us
    all_gather x1, waiting for transfers between devices, per_device(): lax.all_gather(w_outer, 'dp', axis=1, tiled=True)  79.6 us
    all_gather x1, waiting for transfers between devices, per_device(): lax.all_gather(w_inner, 'dp', axis=0, tiled=True)  74.1 us
  transfers between devices with their start and end apart: 22, of which 19 were waited for; matrix products, arithmetic and copies ran while one was open for 11% of the time, Pallas kernels for 0%

commit v1 on v0

--- a/solution.py
+++ b/solution.py
@@ -11,6 +11,19 @@
 L = 1024
 epsilon = 1e-06
 very_negative = -1e30
+
+
+def gather_around(value, axis, dim):
+    ways = lax.axis_size(axis)
+    up = [(d, (d + 1) % ways) for d in range(ways)]
+    down = [(d, (d - 1) % ways) for d in range(ways)]
+    earlier, later = ([value], [value])
+    for _ in range(ways // 2):
+        earlier.append(lax.ppermute(earlier[-1], axis, up))
+    for _ in range((ways - 1) // 2):
+        later.append(lax.ppermute(later[-1], axis, down))
+    line = jnp.concatenate([*earlier[::-1], *later[1:]], axis=dim)
+    return jnp.roll(line, (lax.axis_index(axis) - ways // 2) * value.shape[dim], axis=dim)
 
 
 def rms_norm(matrix_rows, gain_vec):
@@ -138,7 +151,7 @@
     gain_ffn_f = gain_f_full.astype(jnp.float32)
     query_weight, key_w, value_w, output_weight, inner_weight, outer_weight = (
         lax.all_gather(w_query, "dp", axis=0, tiled=True),
-        lax.all_gather(w_key, "dp", axis=0, tiled=True),
+        gather_around(w_key, "dp", 0),
         lax.all_gather(w_value, "dp", axis=0, tiled=True),
         lax.all_gather(w_output, "dp", axis=1, tiled=True),
         lax.all_gather(w_inner, "dp", axis=0, tiled=True),

time: 1570 us -> 1520 us (0.968)
  waiting for transfers between devices: 1140 us -> 1020 us
  starting transfers between devices: 2.01 us -> 44.2 us
  local copies, waits for them, and re-layouts: 35.8 us -> 57.2 us
    all_gather x1, waiting for transfers between devices: 54.7 us -> 0.02 us  [per_device(): lax.all_gather(w_query, 'dp', axis=0, tiled=True)]
    all_gather x1 -> x0, waiting for transfers between devices: 53.1 us -> none  [per_device(): lax.all_gather(w_key, 'dp', axis=0, tiled=True)]
    ppermute x0 -> x15, starting transfers between devices: none -> 43 us  [the longest x7 41.5 us: gather_around(): later.append(lax.ppermute(later[-1], axis, down))]
    unnamed x98 -> x141, local copies, waits for them, and re-layouts: 27.8 us -> 52 us
    all_gather x1, waiting for transfers between devices: 21.9 us -> 0.02 us  [per_device(): lax.all_gather(w_value, 'dp', axis=0, tiled=True)]
    ppermute x0 -> x15, waiting for transfers between devices: none -> 16.5 us  [the longest x8 8.26 us: gather_around(): earlier.append(lax.ppermute(earlier[-1], axis, up))]
    unnamed x23 -> x22, waiting for transfers between devices: 169 us -> 168 us
  transfers between devices with their start and end apart: 22 -> 36, of which waited for: 19 -> 22; matrix products, arithmetic and copies ran while one was open for 11% -> 13% of each run, Pallas kernels for 0% -> 0%
where the time goes in v1:
time: 1520 us; the launch traced here: 1510 us
  waiting for transfers between devices  1020 us (67%)
  matrix products  211 us (14%)
  blocking collectives  86.2 us (6%)
  other arithmetic  74.1 us (5%)
  local copies, waits for them, and re-layouts  57.2 us (4%)
  starting transfers between devices  44.2 us (3%)
  between operations  17.8 us (1%)
    reduce_scatter x1, waiting for transfers between devices, per_device(): lax.psum_scatter(grad_inner_part, 'dp', scatter_dimension=0, tiled=True)  183 us
    reduce_scatter x1, waiting for transfers between devices, per_device(): lax.psum_scatter(grad_outer_part, 'dp', scatter_dimension=1, tiled=True)  177 us
    unnamed x22, waiting for transfers between devices  168 us
    unnamed x3, blocking collectives  86.2 us
    reduce_scatter x1, waiting for transfers between devices, per_device(): lax.psum_scatter(grad_key_part, 'dp', scatter_dimension=0, tiled=True)  81 us
    reduce_scatter x1, waiting for transfers between devices, per_device(): lax.psum_scatter(grad_query_part, 'dp', scatter_dimension=0, tiled=True)  80.8 us
    all_gather x1, waiting for transfers between devices, per_device(): lax.all_gather(w_outer, 'dp', axis=1, tiled=True)  79.4 us
    all_gather x1, waiting for transfers between devices, per_device(): lax.all_gather(w_inner, 'dp', axis=0, tiled=True)  75.2 us
  transfers between devices with their start and end apart: 36, of which 22 were waited for; matrix products, arithmetic and copies ran while one was open for 13% of the time, Pallas kernels for 0%

profile of v1, /device:TPU:0, one launch (start us, length us, event | category | flops | bytes accessed | tf_op | source)
XLA Modules:
  0.0 1510.4 jit_solution(10682774808566057533)
XLA Ops:
  9.7 43.0 %all-reduce.6 = (bf16[1024]{0:T(1024)(128)(2,1)S(1)}, bf16[1024]{0:T(1024)(128)(2,1)S(1)}) all-reduce(bf16[1024]{0:T(1024)(128)(2,1)S(1)} %dynamic-update-slice.1, bf16[1024]{0:T(1024)(128)(2,1)S(1)} %dynamic-update-slice), channel_id=1, replica_groups=mesh['dp'=16,'tensor'=2] {'dp','tensor'}, use_global_device_ids=true, to_apply=%add.1 | all-reduce | flops 2048 | bytes 8192
  56.8 26.3 %all-gather.11.cloned.1.call-done = bf16[3072,1024]{1,0:T(8,128)(2,1)} async-done(((bf16[96,1024]{1,0:T(8,128)(2,1)}), bf16[3072,1024]{1,0:T(8,128)(2,1)}) %all-gather.11.cloned.1.call-update) | async-done | bytes 6291472 | tf_op jit(solution)/shard_map/all_gather | solution.py:146
  83.1 5.1 convolution_bitcast_fusion.1
  94.5 6.4 collective-permute-done
  101.0 5.6 collective-permute-start.8
  110.7 5.7 collective-permute-start.9
  118.5 6.1 collective-permute-start.10
  126.5 6.1 collective-permute-start.11
  134.7 6.2 collective-permute-start.12
  143.3 6.1 collective-permute-start.13
  149.4 4.2 fusion.15
  153.6 5.8 collective-permute-start.14
  184.3 7.0 convolution_convert_fusion
  195.2 14.6 fusion.79
  209.9 13.6 fusion
  223.5 4.9 convolution_convert_fusion.1
  228.4 15.7 %fusion.49 = bf16[4,128,1024]{2,1,0:T(8,128)(2,1)} fusion(bf16[2048,4,128]{0,2,1:T(8,128)(2,1)S(1)} %bitcast.131, f32[4,1024,2048]{2,1,0:T(8,128)} %get-tuple-element.112, f32[4,1024]{1,0:T(4,128)S(1)} %fusion, f32[4,1024]{1,0:T(4,128)S(1)} %get-tuple-element.111), kind=kOutput, calls=%fused_computation.82 | convolution fusion | flops 2173173760 | bytes 36732928 | tf_op jit(solution)/shard_map/while/body/eval_jaxpr/hqk,khd->qhd/dot_general | solution.py:65
  244.1 34.5 %all-gather.19.cloned.1.call-done = bf16[512,1024]{0,1:T(8,128)(2,1)} async-done(((bf16[512,64]{0,1:T(8,128)(2,1)}), bf16[512,1024]{0,1:T(8,128)(2,1)}) %all-gather.19.cloned.1.call-update) | async-done | bytes 1048592 | tf_op jit(solution)/shard_map/all_gather | solution.py:156
  283.6 7.9 reduce-scatter.15.cloned.1.call-done
  296.0 75.2 %all-gather.23.cloned.1.call-done = bf16[1024,2048]{1,0:T(8,128)(2,1)} async-done(((bf16[64,2048]{1,0:T(8,128)(2,1)}), bf16[1024,2048]{1,0:T(8,128)(2,1)}) %all-gather.23.cloned.1.call-update) | async-done | bytes 4194320 | tf_op jit(solution)/shard_map/all_gather | solution.py:157
  371.2 11.3 all-gather.21.cloned.1.call-done
  382.5 10.9 fusion.44
  395.9 79.4 %all-gather.25.cloned.1.call-done = bf16[2048,1024]{0,1:T(8,128)(2,1)} async-done(((bf16[2048,64]{0,1:T(8,128)(2,1)}), bf16[2048,1024]{0,1:T(8,128)(2,1)}) %all-gather.25.cloned.1.call-update) | async-done | bytes 4194320 | tf_op jit(solution)/shard_map/all_gather | solution.py:158
  475.3 13.0 fusion.12
  490.4 5.8 convert_bitcast_fusion
  496.2 11.1 convert_bitcast_fusion.1
  507.6 10.3 reduce-scatter.17.cloned.1.call-done
  517.9 5.2 fusion.29
  525.5 11.9 all-gather.29.cloned.1.call-done
  540.6 15.1 %fusion.21 = bf16[4,128,2048]{2,1,0:T(8,128)(2,1)} fusion(bf16[1024,4,128]{0,2,1:T(8,128)(2,1)S(1)} %bitcast.125, f32[4,1024,2048]{2,1,0:T(8,128)} %get-tuple-element.112, f32[4,1024]{1,0:T(4,128)S(1)} %log_add_fusion), kind=kOutput, calls=%fused_computation.43 | convolution fusion | flops 2165309440 | bytes 36716544 | tf_op jit(solution)/shard_map/while/body/eval_jaxpr/hqk,qhd->khd/dot_general | solution.py:74
  555.7 22.0 %multiply_reduce_fusion = (f32[4,1024]{1,0:T(4,128)S(1)}, f32[4,1024,2048]{2,1,0:T(8,128)}) fusion(f32[4,1024,2048]{2,1,0:T(8,128)} %get-tuple-element.112, f32[4,1024]{1,0:T(4,128)S(1)} %log_add_fusion, bf16[1024,4,128]{0,2,1:T(8,128)(2,1)S(1)} %bitcast.126, bf16[2048,4,128]{0,2,1:T(8,128)(2,1)S(1)} %bitcast.132), kind=kOutput, calls=%fused_computation.1 | convolution fusion | flops 2172645376 | bytes 70287360 | tf_op jit(solution)/shard_map/while/body/eval_jaxpr/qhd,khd->hqk/dot_general | solution.py:73
  577.7 28.2 %multiply_convert_fusion = bf16[4,1024,2048]{2,1,0:T(8,128)(2,1)} fusion(f32[4,1024,2048]{2,1,0:T(8,128)} %get-tuple-element.114, f32[4,1024,2048]{2,1,0:T(8,128)} %get-tuple-element.112, f32[4,1024]{1,0:T(4,128)S(1)} %get-tuple-element.113, f32[4,1024]{1,0:T(4,128)S(1)} %log_add_fusion), kind=kLoop, calls=%fused_computation | loop fusion | flops 33554432 | bytes 83918848 | tf_op jit(solution)/shard_map/while/body/eval_jaxpr/convert_element_type | solution.py:79
  606.0 11.4 multiply_convert_fusion.4
  617.4 8.7 multiply_convert_fusion.2
  637.5 4.5 fusion.32
  642.2 6.8 fusion.74
  649.1 6.1 fusion.75
  661.0 11.3 fusion.36
  673.9 9.0 fusion.42
  691.7 6.4 convolution_bitcast_fusion
  698.2 12.7 copy.41
  717.9 40.8 %all-reduce.5 = (f32[1024]{0:T(1024)S(1)}, f32[1024]{0:T(1024)S(1)}) all-reduce(f32[1024]{0:T(1024)S(1)} %get-tuple-element.93, f32[1024]{0:T(1024)S(1)} %copy-done.43), channel_id=11, replica_groups=mesh['dp'=16,'tensor'=2] {'dp','tensor'}, use_global_device_ids=true, to_apply=%region_17.18.clone | all-reduce | flops 2048 | bytes 16384
  763.6 53.5 %reduce-scatter.27.cloned.1.call-done = f32[64,512]{1,0:T(8,128)} async-done(((f32[1024,512]{1,0:T(8,128)}), f32[64,512]{1,0:T(8,128)}) %reduce-scatter.27.cloned.1.call-update) | async-done | bytes 131088 | tf_op jit(solution)/shard_map/reduce_scatter | solution.py:304
  817.1 81.0 %reduce-scatter.25.cloned.1.call-done = f32[64,512]{1,0:T(8,128)} async-done(((f32[1024,512]{1,0:T(8,128)}), f32[64,512]{1,0:T(8,128)}) %reduce-scatter.25.cloned.1.call-update) | async-done | bytes 131088 | tf_op jit(solution)/shard_map/reduce_scatter | solution.py:303
  898.1 80.8 %reduce-scatter.23.cloned.1.call-done = f32[64,512]{1,0:T(8,128)} async-done(((f32[1024,512]{1,0:T(8,128)}), f32[64,512]{1,0:T(8,128)}) %reduce-scatter.23.cloned.1.call-update) | async-done | bytes 131088 | tf_op jit(solution)/shard_map/reduce_scatter | solution.py:302
  979.0 177.3 %reduce-scatter.33.cloned.1.call-done = f32[2048,64]{0,1:T(8,128)} async-done(((f32[2048,1024]{0,1:T(8,128)}), f32[2048,64]{0,1:T(8,128)}) %reduce-scatter.33.cloned.1.call-update) | async-done | bytes 524304 | tf_op jit(solution)/shard_map/reduce_scatter | solution.py:307
  1156.3 183.0 %reduce-scatter.31.cloned.1.call-done = f32[64,2048]{1,0:T(8,128)} async-done(((f32[1024,2048]{1,0:T(8,128)}), f32[64,2048]{1,0:T(8,128)}) %reduce-scatter.31.cloned.1.call-update) | async-done | bytes 524304 | tf_op jit(solution)/shard_map/reduce_scatter | solution.py:306
  1339.4 164.0 %reduce-scatter.35.cloned.1.call-done = f32[96,1024]{1,0:T(8,128)} async-done(((f32[3072,1024]{1,0:T(8,128)}), f32[96,1024]{1,0:T(8,128)}) %reduce-scatter.35.cloned.1.call-update) | async-done | bytes 393232
  (251 shorter events, 111.1 us)
Async XLA Ops:
  7.2 47.7 %copy-start.25 = (bf16[1,768,1024]{2,1,0:T(8,128)(2,1)S(1)}, bf16[1,768,1024]{2,1,0:T(8,128)(2,1)}, u32[]{:S(2)}) copy-start(bf16[1,768,1024]{2,1,0:T(8,128)(2,1)} %param.17) | copy-start | bytes 4718596
  7.2 75.9 %all-gather.11.cloned.1.call-start = ((), (), s32[]{:S(2)}) async-start(), calls=%async_computation.11 | async-start | bytes 6488064 | tf_op jit(solution)/shard_map/all_gather | solution.py:146
  7.9 171.6 %all-gather.13.cloned.1.call-start = ((), (), s32[]{:S(2)}) async-start(), calls=%async_computation.12 | async-start | bytes 6291456 | tf_op jit(solution)/shard_map/all_gather | solution.py:168
  52.7 36.5 %copy-start.33 = (f32[1024]{0:T(1024)}, f32[1024]{0:T(1024)S(1)}, u32[]{:S(2)}) copy-start(f32[1024]{0:T(1024)S(1)} %convert_element_type.166) | copy-start | bytes 12292
  56.8 32.5 %copy-start = (f32[1,512,1024]{2,1,0:T(8,128)}, f32[1,512,1024]{2,1,0:T(8,128)S(1)}, u32[]{:S(2)}) copy-start(f32[1,512,1024]{2,1,0:T(8,128)S(1)} %convert_element_type.164) | copy-start | bytes 6291460
  91.7 99.6 %all-gather.17.cloned.1.call-start = ((), (), s32[]{:S(2)}) async-start(), calls=%async_computation.14 | async-start | bytes 1114112 | tf_op jit(solution)/shard_map/all_gather | solution.py:153
  92.4 131.1 %all-gather.15.cloned.1.call-start = ((), (), s32[]{:S(2)}) async-start(), calls=%async_computation.13 | async-start | bytes 1114112 | tf_op jit(solution)/shard_map/all_gather | solution.py:155
  93.0 185.6 %all-gather.19.cloned.1.call-start = ((), (), s32[]{:S(2)}) async-start(), calls=%async_computation.15 | async-start | bytes 1114112 | tf_op jit(solution)/shard_map/all_gather | solution.py:156
  93.0 7.9 collective-permute-start
  101.0 7.9 collective-permute-start.1
  101.0 9.8 collective-permute-start.8
  106.6 184.9 %reduce-scatter.15.cloned.1.call-start = ((), (), s32[]{:S(2)}) async-start(), calls=%async_computation.16 | async-start | bytes 3145728 | tf_op jit(solution)/shard_map/reduce_scatter | solution.py:190
  108.8 7.9 collective-permute-start.2
  110.7 7.7 collective-permute-start.9
  116.7 7.9 collective-permute-start.3
  118.5 8.1 collective-permute-start.10
  124.6 8.0 collective-permute-start.4
  126.5 8.1 collective-permute-start.11
  132.6 8.2 collective-permute-start.5
  134.7 8.6 collective-permute-start.12
  140.8 8.6 collective-permute-start.6
  143.3 10.3 collective-permute-start.13
  149.4 9.9 collective-permute-start.7
  153.6 15.2 %collective-permute-start.14 = (bf16[64,512]{1,0:T(8,128)(2,1)S(1)}, bf16[64,512]{1,0:T(8,128)(2,1)S(1)}, u32[]{:S(2)}, u32[]{:S(2)}) collective-permute-start(bf16[64,512]{1,0:T(8,128)(2,1)S(1)} %collective-permute-done.13), channel_id=1, source_target_pairs={{0,30},{2,0},{4,2},{6,4},{8,6},{10,8},{12,10},{14,12},{16,14},{18,... | collective-permute-start | bytes 196616 | tf_op jit(solution)/shard_map/ppermute | solution.py:24
  282.8 88.4 %all-gather.23.cloned.1.call-start = ((), (), s32[]{:S(2)}) async-start(), calls=%async_computation.18 | async-start | bytes 4456448 | tf_op jit(solution)/shard_map/all_gather | solution.py:157
  283.5 99.0 %all-gather.21.cloned.1.call-start = ((), (), s32[]{:S(2)}) async-start(), calls=%async_computation.17 | async-start | bytes 3145728 | tf_op jit(solution)/shard_map/all_gather | solution.py:196
  283.6 239.5 %copy-start.31 = (f32[1024]{0:T(1024)}, f32[1024]{0:T(1024)S(1)}, u32[]{:S(2)}) copy-start(f32[1024]{0:T(1024)S(1)} %convert_element_type.177) | copy-start | bytes 12292
  293.3 229.8 %copy-start.37 = (f32[512]{0:T(512)}, f32[512]{0:T(512)S(1)}, u32[]{:S(2)}) copy-start(f32[512]{0:T(512)S(1)} %fusion.68) | copy-start | bytes 6148
  294.7 101.2 %all-gather.27.cloned.1.call-start = ((), (), s32[]{:S(2)}) async-start(), calls=%async_computation.21 | async-start | bytes 3145728 | tf_op jit(solution)/shard_map/all_gather | solution.py:218
  295.4 179.9 %all-gather.25.cloned.1.call-start = ((), (), s32[]{:S(2)}) async-start(), calls=%async_computation.19 | async-start | bytes 4456448 | tf_op jit(solution)/shard_map/all_gather | solution.py:158
  296.0 211.6 %reduce-scatter.19.cloned.1.call-start = ((), (), s32[]{:S(2)}) async-start(), calls=%async_computation.22 | async-start | bytes 3145728 | tf_op jit(solution)/shard_map/reduce_scatter | solution.py:234
  496.2 21.7 %reduce-scatter.17.cloned.1.call-start = ((), (), s32[]{:S(2)}) async-start(), calls=%async_computation.20 | async-start | bytes 3145728 | tf_op jit(solution)/shard_map/reduce_scatter | solution.py:205
  507.3 30.1 %all-gather.29.cloned.1.call-start = ((), (), s32[]{:S(2)}) async-start(), calls=%async_computation.23 | async-start | bytes 3145728 | tf_op jit(solution)/shard_map/all_gather | solution.py:244
  525.5 157.5 %reduce-scatter.21.cloned.1.call-start = ((), (), s32[]{:S(2)}) async-start(), calls=%async_computation.24 | async-start | bytes 6291456 | tf_op jit(solution)/shard_map/reduce_scatter | solution.py:287
  577.7 28.2 %copy-start.17 = (bf16[2048,512]{0,1:T(8,128)(2,1)S(1)}, bf16[2048,512]{0,1:T(8,128)(2,1)}, u32[]{:S(2)}) copy-start(bf16[2048,512]{0,1:T(8,128)(2,1)} %copy-done.16) | copy-start | bytes 6291460
  637.5 126.1 %reduce-scatter.29.cloned.1.call-start = ((), (), s32[]{:S(2)}) async-start(), calls=%async_computation.28 | async-start | bytes 2228224 | tf_op jit(solution)/shard_map/reduce_scatter | solution.py:305
  642.1 175.0 %reduce-scatter.27.cloned.1.call-start = ((), (), s32[]{:S(2)}) async-start(), calls=%async_computation.27 | async-start | bytes 2228224 | tf_op jit(solution)/shard_map/reduce_scatter | solution.py:304
  649.0 249.1 %reduce-scatter.25.cloned.1.call-start = ((), (), s32[]{:S(2)}) async-start(), calls=%async_computation.26 | async-start | bytes 2228224 | tf_op jit(solution)/shard_map/reduce_scatter | solution.py:303
  655.2 323.8 %reduce-scatter.23.cloned.1.call-start = ((), (), s32[]{:S(2)}) async-start(), calls=%async_computation.25 | async-start | bytes 2228224 | tf_op jit(solution)/shard_map/reduce_scatter | solution.py:302
  659.4 496.9 %reduce-scatter.33.cloned.1.call-start = ((), (), s32[]{:S(2)}) async-start(), calls=%async_computation.30 | async-start | bytes 8912896 | tf_op jit(solution)/shard_map/reduce_scatter | solution.py:307
  672.4 667.0 %reduce-scatter.31.cloned.1.call-start = ((), (), s32[]{:S(2)}) async-start(), calls=%async_computation.29 | async-start | bytes 8912896 | tf_op jit(solution)/shard_map/reduce_scatter | solution.py:306
  682.9 820.4 %reduce-scatter.35.cloned.1.call-start = ((), (), s32[]{:S(2)}) async-start(), calls=%async_computation.31 | async-start | bytes 12976128
  710.9 49.0 %copy-start.3 = (bf16[1,512,1024]{2,1,0:T(8,128)(2,1)S(1)}, bf16[1,512,1024]{2,1,0:T(8,128)(2,1)}, u32[]{:S(2)}) copy-start(bf16[1,512,1024]{2,1,0:T(8,128)(2,1)} %param.15) | copy-start | bytes 3145732
  710.9 49.0 %copy-start.5 = (bf16[1,512,1024]{2,1,0:T(8,128)(2,1)S(1)}, bf16[1,512,1024]{2,1,0:T(8,128)(2,1)}, u32[]{:S(2)}) copy-start(bf16[1,512,1024]{2,1,0:T(8,128)(2,1)} %reduce-scatter.15.cloned.1.call-done) | copy-start | bytes 3145732
  710.9 49.0 %copy-start.12 = (bf16[1,512,1024]{2,1,0:T(8,128)(2,1)S(1)}, bf16[1,512,1024]{2,1,0:T(8,128)(2,1)}, u32[]{:S(2)}) copy-start(bf16[1,512,1024]{2,1,0:T(8,128)(2,1)} %param.29) | copy-start | bytes 3145732
  710.9 49.0 %copy-start.32 = (f32[1024]{0:T(1024)S(1)}, f32[1024]{0:T(1024)}, u32[]{:S(2)}) copy-start(f32[1024]{0:T(1024)} %copy-done.31) | copy-start | bytes 12292
  710.9 49.0 %copy-start.38 = (f32[512]{0:T(512)S(1)}, f32[512]{0:T(512)}, u32[]{:S(2)}) copy-start(f32[512]{0:T(512)} %copy-done.37) | copy-start | bytes 6148
  710.9 49.0 %copy-start.42 = (f32[512]{0:T(512)S(1)}, f32[512]{0:T(512)}, u32[]{:S(2)}) copy-start(f32[512]{0:T(512)} %copy-done.41) | copy-start | bytes 6148
  (39 other events, 187.6 us)
Sparse Core Ops, SparseCore 0:
  10.9 72.2 all-gather.10
  91.8 12.1 all-gather.12
  106.8 57.2 all-gather.16
  166.7 55.2 all-gather.14
  224.6 53.9 all-gather.18
  282.9 8.5 reduce-scatter.14
  294.3 76.8 all-gather.22
  373.3 9.1 all-gather.20
  384.1 11.7 all-gather.26
  398.5 76.7 all-gather.24
  496.3 8.3 reduce-scatter.18
  507.4 10.3 reduce-scatter.16
  525.6 11.8 all-gather.28
  637.6 13.2 reduce-scatter.20
  653.6 82.7 reduce-scatter.28
  739.0 78.0 reduce-scatter.26
  819.8 78.2 reduce-scatter.24
  900.8 78.0 reduce-scatter.22
  981.9 174.4 reduce-scatter.32
  1159.0 180.2 reduce-scatter.30
  1346.0 157.3 reduce-scatter.34
